TPU v7x, 32 devices: a whole 2x2x4 slice. The times are simulated.
32 devices in a mesh: grp: 2 (over x), exp: 16 (over z, y, core).
Axes of the slice: x: 2, y: 2, z: 4, core: 2. Of those that a mesh axis runs over, the one named last changes fastest.
Arguments:
- hidden: bfloat16 [32, 4096], P(('grp', 'exp')), may hold values from -6 to 6
- route_ids: int32 [32, 8], P(('grp', 'exp')), may hold values from 0 to 15, all different within a row; in each aligned block of 32 rows (0 to 31, 32 to 63, ...) at most 32 rows name the same one
- route_logits: bfloat16 [32, 8], P(('grp', 'exp')), may hold values from -6 to 6
- sampled: int32 [32], P(('grp', 'exp')), may hold values from 0 to 131071
- norm_gain: float32 [4096], replicated, may hold values from 0.5 to 1.5
- gate_weight: bfloat16 [16, 4096, 1536], P('exp', 'grp'), may hold values from -0.09375 to 0.09375
- up_weight: bfloat16 [16, 4096, 1536], P('exp', 'grp'), may hold values from -0.09375 to 0.09375
- down_weight: bfloat16 [16, 1536, 4096], P('exp', None, 'grp'), may hold values from -0.15625 to 0.15625
- head_weight: bfloat16 [4096, 131072], P(None, ('grp', 'exp')), may hold values from -0.25 to 0.25
- noise_steps: int32 [131072], P(('grp', 'exp')), may hold values from -64 to 64
Outputs:
- vote_counts: float32 [131072], P(('grp', 'exp'))
- log_ratio: float32 [32], P(('grp', 'exp'))
Inputs may be any that keep to these rules, and one draw needn't show every extreme that they name: `route_ids`: each row names 8 different experts. Over all 32 rows no expert is named by more than 32 rows, a bound that some block reaches.
All inputs are finite; a program needn't handle non-finite values.
Results may differ from a plain program's by a relative error of at most 0.004.
Values may be sent and summed in bfloat16 or wider, within the bound.
A program may use at most 128 MiB of HBM per device.

v0:
```python
import jax
import jax.numpy as jnp
from jax import lax
from jax.sharding import PartitionSpec as P

TOPK = 8
VOCAB = 131072


clip_bound = 8.0
noise_step = 0.03125
norm_eps = 1e-06


def on_device(
    hidden,
    route_ids,
    route_logits,
    sampled,
    norm_gain,
    gate_weight,
    up_weight,
    down_weight,
    head_weight,
    noise_steps,
):
    groups = lax.axis_size("grp")
    columns_count = lax.axis_size("exp")
    width = gate_weight.shape[1]
    column_index = lax.axis_index("exp")
    device_index = lax.axis_index(("grp", "exp"))
    group_rows, group_ids, group_logits, group_sampled = (
        lax.all_gather(hidden, "exp", axis=0, tiled=True),
        lax.all_gather(route_ids, "exp", axis=0, tiled=True),
        lax.all_gather(route_logits, "exp", axis=0, tiled=True),
        lax.all_gather(sampled, "exp", axis=0, tiled=True),
    )
    row_count = group_rows.shape[0]
    topk_width = group_ids.shape[1]
    pieces = group_rows.reshape(row_count, groups, width)
    ids_spread = jnp.broadcast_to(group_ids[:, None, :], (row_count, groups, topk_width))
    logits_spread = jnp.broadcast_to(group_logits[:, None, :], (row_count, groups, topk_width))
    sampled_spread = jnp.broadcast_to(group_sampled[:, None, None], (row_count, groups, 1))
    arrived = (
        lax.all_to_all(pieces, "grp", split_axis=1, concat_axis=0, tiled=True),
        lax.all_to_all(ids_spread, "grp", split_axis=1, concat_axis=0, tiled=True),
        lax.all_to_all(logits_spread, "grp", split_axis=1, concat_axis=0, tiled=True),
        lax.all_to_all(sampled_spread, "grp", split_axis=1, concat_axis=0, tiled=True),
    )
    member_count = row_count * groups
    width_slab = arrived[0].reshape(member_count, width)
    ids_all = arrived[1].reshape(member_count, topk_width)
    logits_all = arrived[2].reshape(member_count, topk_width)
    sampled_all = arrived[3].reshape(member_count)
    members_total = width_slab.shape[0]
    capacity = min(members_total, 2 * members_total * TOPK // columns_count)
    mixing = jax.nn.softmax(logits_all.astype(jnp.float32), axis=-1)
    matches = ids_all == column_index
    chosen = jnp.any(matches, axis=1)
    share = jnp.sum(jnp.where(matches, mixing, 0.0), axis=1)
    position = jnp.cumsum(chosen.astype(jnp.int32)) - 1
    slot_index = jnp.arange(capacity, dtype=jnp.int32)
    select = ((position[None, :] == slot_index[:, None]) & chosen[None, :]).astype(jnp.bfloat16)
    picked = jnp.dot(select, width_slab, preferred_element_type=jnp.float32).astype(jnp.bfloat16)
    gate_part = jnp.dot(picked, gate_weight[0], preferred_element_type=jnp.float32)
    upward_part = jnp.dot(picked, up_weight[0], preferred_element_type=jnp.float32)
    gate_sum, upward_sum = lax.psum((gate_part, upward_part), "grp")
    active = (jax.nn.silu(gate_sum) * upward_sum).astype(jnp.bfloat16)
    output = jnp.dot(active, down_weight[0], preferred_element_type=jnp.float32).astype(
        jnp.bfloat16
    )
    spread = jnp.einsum("cm,cw->mw", select, output, preferred_element_type=jnp.float32)
    contrib = spread * share[:, None]
    moe_slab = lax.psum(contrib, "exp")
    residual = (width_slab.astype(jnp.float32) + moe_slab).astype(jnp.bfloat16)
    vocab_block = head_weight.shape[1]
    piece = lax.all_gather(residual, "grp", axis=1, tiled=True)
    scaled = (piece.astype(jnp.float32) * norm_gain[None, :]).astype(jnp.bfloat16)
    acc_logits = jnp.dot(scaled, head_weight, preferred_element_type=jnp.float32)
    acc_squares = jnp.sum(jnp.square(piece.astype(jnp.float32)), axis=1)
    model_width = norm_gain.shape[0]
    root_mean = jnp.sqrt(acc_squares / model_width + norm_eps)
    logits = acc_logits / root_mean[:, None]
    clipped = jnp.clip(logits, -clip_bound, clip_bound)
    exp_values = jnp.exp(clipped)
    first_column = device_index * vocab_block
    vocab_columns = first_column + jnp.arange(vocab_block, dtype=jnp.int32)
    owned = sampled_all[:, None] == vocab_columns[None, :]
    part_total = jnp.sum(exp_values, axis=1)
    part_chosen = jnp.sum(jnp.where(owned, clipped, 0.0), axis=1)
    totals, chosen_logit = lax.psum((part_total, part_chosen), ("grp", "exp"))
    log_ratio = chosen_logit - jnp.log(totals / VOCAB)
    own_rows = hidden.shape[0]
    own_ratio = lax.dynamic_slice_in_dim(log_ratio, device_index * own_rows, own_rows, 0)
    vote_counts = (
        VOCAB / members_total * jnp.sum(exp_values / totals[:, None], axis=0)
        + noise_steps.astype(jnp.float32) * noise_step
    )
    return (vote_counts, own_ratio)


def solution(mesh):
    placed = (
        P(("grp", "exp"), None),
        P(("grp", "exp"), None),
        P(("grp", "exp"), None),
        P(("grp", "exp")),
        P(),
        P("exp", "grp", None),
        P("exp", "grp", None),
        P("exp", None, "grp"),
        P(None, ("grp", "exp")),
        P(("grp", "exp")),
    )
    return jax.shard_map(
        on_device,
        mesh=mesh,
        in_specs=placed,
        out_specs=(P(("grp", "exp")), P(("grp", "exp"))),
        check_vma=False,
    )
```

profile of v0, /device:TPU:0, one launch (start us, length us, event | category | flops | bytes accessed | tf_op | source)
XLA Modules:
  0.0 297.2 jit_solution(6315251923228911917)
XLA Ops:
  7.2 23.3 %all-gather.1 = s32[16,1,8]{2,1,0:T(1,128)S(1)} all-gather(s32[1,1,8]{2,1,0:T(1,128)} %bitcast.59), channel_id=1, replica_groups=mesh['grp'=2,'exp'=16] {'exp'}, dimensions={0}, use_global_device_ids=true | all-gather | bytes 544 | tf_op jit(solution)/shard_map/all_gather | solution.py:34
  30.5 0.6 reshape.123
  31.2 3.2 %all-to-all-start.1 = ((s32[2,1,128]{2,1,0:T(1,128)}), s32[2,1,128]{2,1,0:T(1,128)S(1)}, u32[]{:S(2)}, u32[]{:S(2)}) async-start(s32[2,1,128]{2,1,0:T(1,128)} %reshape.123), calls=%async_computation.1 | async-start | bytes 2048 | tf_op jit(solution)/shard_map/all_to_all | solution.py:46
  34.4 18.4 %all-gather = bf16[16,1,4096]{2,1,0:T(2,128)(2,1)S(1)} all-gather(bf16[1,1,4096]{2,1,0:T(2,128)(2,1)} %bitcast.55), channel_id=1, replica_groups=mesh['grp'=2,'exp'=16] {'exp'}, dimensions={0}, use_global_device_ids=true | all-gather | bytes 139264 | tf_op jit(solution)/shard_map/all_gather | solution.py:33
  52.8 0.7 reduce.5
  53.5 0.6 copy.29
  54.2 3.4 %all-to-all-start = ((bf16[16,2,2048]{2,0,1:T(8,128)(2,1)}), bf16[16,2,2048]{2,0,1:T(8,128)(2,1)S(1)}, u32[]{:S(2)}, u32[]{:S(2)}) async-start(bf16[16,2,2048]{2,0,1:T(8,128)(2,1)} %bitcast.52), calls=%async_computation | async-start | bytes 262144 | tf_op jit(solution)/shard_map/all_to_all | solution.py:45
  57.6 0.5 broadcast.52
  58.1 0.7 reduce.8
  59.2 2.9 all-to-all-done
  62.1 0.2 convolution_convert_fusion
  62.3 4.8 %fusion.2 = f32[32,1536]{1,0:T(8,128)} fusion(bf16[32,2048]{1,0:T(8,128)(2,1)S(1)} %convolution_convert_fusion, bf16[1,2048,1536]{2,1,0:T(8,128)(2,1)} %param.16), kind=kOutput, calls=%fused_computation.2 | convolution fusion | flops 201326592 | bytes 6619136 | tf_op jit(solution)/shard_map/dot_general | solution.py:66
  67.0 1.8 fusion.4
  68.9 19.2 %all-gather.2 = bf16[16,1,8]{2,1,0:T(2,128)(2,1)S(1)} all-gather(bf16[1,1,8]{2,1,0:T(2,128)(2,1)S(1)} %bitcast.60), channel_id=1, replica_groups=mesh['grp'=2,'exp'=16] {'exp'}, dimensions={0}, use_global_device_ids=true | all-gather | bytes 272 | tf_op jit(solution)/shard_map/all_gather | solution.py:35
  88.2 6.1 %all_to_all.54 = bf16[16,2,8]{0,2,1:T(8,128)(2,1)S(1)} all-to-all(bf16[16,2,8]{0,2,1:T(8,128)(2,1)S(1)} %broadcast_in_dim.13), channel_id=1, replica_groups=mesh['grp'=2,'exp'=16] {'grp'}, dimensions={1} | all-to-all | bytes 1024 | tf_op jit(solution)/shard_map/all_to_all | solution.py:47
  94.5 5.0 %convolution_multiply_fusion = f32[32,2048]{1,0:T(8,128)} fusion(bf16[1,1536,2048]{2,1,0:T(8,128)(2,1)} %param.17, f32[32]{0:T(128)S(1)} %mul.45, f32[32,1536]{1,0:T(8,128)} %get-tuple-element.4, f32[32,1536]{1,0:T(8,128)} %get-tuple-element.5, s32[32]{0:T(128)S(1)} %add_reduce_fusion, pred[32]{0:T(512)(128)(4,1)S(1)} %and.12), kind=kOutput, calls=%fused_computation.8 | convolution fusion | flops 205948928 | bytes 6947104 | tf_op jit(solution)/shard_map/cm,cw->mw/dot_general | solution.py:72
  100.2 0.6 dynamic-slice
  100.8 0.8 dynamic-update-slice
  101.5 10.2 %all-reduce = s32[16]{0:T(128)S(1)} all-reduce(s32[16]{0:T(128)S(1)} %dynamic-update-slice), channel_id=1, replica_groups=mesh['grp'=2,'exp'=16] {'exp'}, use_global_device_ids=true, to_apply=%add | all-reduce | flops 16 | bytes 128
  111.7 0.6 broadcast_in_dim.16
  112.3 3.2 %all-to-all-start.3 = ((s32[16,2,1]{0,2,1:T(1,128)}), s32[16,2,1]{0,2,1:T(1,128)S(1)}, u32[]{:S(2)}, u32[]{:S(2)}) async-start(s32[16,2,1]{0,2,1:T(1,128)} %broadcast_in_dim.16), calls=%async_computation.3 | async-start | bytes 2048 | tf_op jit(solution)/shard_map/all_to_all | solution.py:48
  115.5 3.7 %all-to-all-done.3 = s32[16,2,1]{0,2,1:T(1,128)S(1)} async-done(((s32[16,2,1]{0,2,1:T(1,128)}), s32[16,2,1]{0,2,1:T(1,128)S(1)}, u32[]{:S(2)}, u32[]{:S(2)}) %all-to-all-start.3) | async-done | bytes 160 | tf_op jit(solution)/shard_map/all_to_all | solution.py:48
  119.3 68.5 %all-reduce.5.cloned.1.call-done = f32[32,2048]{1,0:T(8,128)} async-done(((f32[32,2048]{1,0:T(8,128)}), f32[32,2048]{1,0:T(8,128)}) %all-reduce.5.cloned.1.call-update) | async-done | bytes 262160 | tf_op jit(solution)/shard_map/psum | solution.py:74
  187.8 1.0 add_convert_fusion
  188.8 6.5 %all_gather.18 = bf16[32,4096]{1,0:T(8,128)(2,1)S(1)} all-gather(bf16[32,2048]{1,0:T(8,128)(2,1)S(1)} %add_convert_fusion), channel_id=1, replica_groups=mesh['grp'=2,'exp'=16] {'grp'}, dimensions={1}, use_global_device_ids=true | all-gather | bytes 393216 | tf_op jit(solution)/shard_map/all_gather | solution.py:77
  195.3 0.2 fusion.13
  195.5 13.7 %exponential_reduce_fusion = (f32[32]{0:T(128)S(1)}, f32[32,4096]{1,0:T(8,128)S(1)}) fusion(f32[32]{0:T(128)S(1)} %add_sqrt_fusion, bf16[4096,4096]{1,0:T(8,128)(2,1)} %param.18, bf16[32,4096]{1,0:T(8,128)(2,1)S(1)} %all_gather.18, f32[4096]{0:T(1024)S(1)} %copy-done.1), kind=kOutput, calls=%fused_computation.17 | convolution fusion | flops 1074528256 | bytes 34357504 | tf_op jit(solution)/shard_map/dot_general | solution.py:79
  209.2 39.8 %psum.38 = f32[32]{0:T(128)S(1)} all-reduce(f32[32]{0:T(128)S(1)} %get-tuple-element.8), channel_id=1, replica_groups=mesh['grp'=2,'exp'=16] {'grp','exp'}, use_global_device_ids=true, to_apply=%region_10.11 | all-reduce | flops 32 | bytes 256 | tf_op jit(solution)/shard_map/psum | solution.py:91
  249.0 0.2 select_reduce_fusion
  249.2 39.9 %psum.39 = f32[32]{0:T(128)S(1)} all-reduce(f32[32]{0:T(128)S(1)} %get-tuple-element.2), channel_id=1, replica_groups=mesh['grp'=2,'exp'=16] {'grp','exp'}, use_global_device_ids=true, to_apply=%region_13.14 | all-reduce | flops 32 | bytes 256 | tf_op jit(solution)/shard_map/psum | solution.py:91
  289.1 0.6 multiply_add_fusion
  289.8 0.6 dynamic_slice.3
  (37 shorter events, 1.0 us)
Async XLA Ops:
  31.2 23.0 %all-to-all-start.1 = ((s32[2,1,128]{2,1,0:T(1,128)}), s32[2,1,128]{2,1,0:T(1,128)S(1)}, u32[]{:S(2)}, u32[]{:S(2)}) async-start(s32[2,1,128]{2,1,0:T(1,128)} %reshape.123), calls=%async_computation.1 | async-start | bytes 2048 | tf_op jit(solution)/shard_map/all_to_all | solution.py:46
  54.2 7.9 %all-to-all-start = ((bf16[16,2,2048]{2,0,1:T(8,128)(2,1)}), bf16[16,2,2048]{2,0,1:T(8,128)(2,1)S(1)}, u32[]{:S(2)}, u32[]{:S(2)}) async-start(bf16[16,2,2048]{2,0,1:T(8,128)(2,1)} %bitcast.52), calls=%async_computation | async-start | bytes 262144 | tf_op jit(solution)/shard_map/all_to_all | solution.py:45
  57.6 36.9 %all-reduce.7.cloned.1.call-start = ((), (), s32[]{:S(2)}) async-start(), calls=%async_computation.5 | async-start | bytes 786432 | tf_op jit(solution)/shard_map/psum | solution.py:67
  62.1 4.9 %copy-start = (bf16[1,2048,1536]{2,1,0:T(8,128)(2,1)S(1)}, bf16[1,2048,1536]{2,1,0:T(8,128)(2,1)}, u32[]{:S(2)}) copy-start(bf16[1,2048,1536]{2,1,0:T(8,128)(2,1)} %param.15) | copy-start | bytes 18874372
  62.3 6.7 %copy-start.3 = (bf16[1,8]{1,0:T(2,128)(2,1)S(1)}, bf16[1,8]{1,0:T(2,128)(2,1)}, u32[]{:S(2)}) copy-start(bf16[1,8]{1,0:T(2,128)(2,1)} %param.12) | copy-start | bytes 52
  67.0 33.1 %copy-start.4 = (u32[32]{0:T(128)S(1)}, u32[32]{0:T(128)}, u32[]{:S(2)}) copy-start(u32[32]{0:T(128)} %constant.59) | copy-start | bytes 388
  67.0 128.4 %copy-start.1 = (f32[4096]{0:T(1024)S(1)}, f32[4096]{0:T(1024)}, u32[]{:S(2)}) copy-start(f32[4096]{0:T(1024)} %param.14) | copy-start | bytes 49156
  68.9 118.9 %all-reduce.5.cloned.1.call-start = ((), (), s32[]{:S(2)}) async-start(), calls=%async_computation.4 | async-start | bytes 524288 | tf_op jit(solution)/shard_map/psum | solution.py:74
  112.3 6.9 %all-to-all-start.3 = ((s32[16,2,1]{0,2,1:T(1,128)}), s32[16,2,1]{0,2,1:T(1,128)S(1)}, u32[]{:S(2)}, u32[]{:S(2)}) async-start(s32[16,2,1]{0,2,1:T(1,128)} %broadcast_in_dim.16), calls=%async_computation.3 | async-start | bytes 2048 | tf_op jit(solution)/shard_map/all_to_all | solution.py:48
  195.5 93.7 %copy-start.2 = (s32[4096]{0:T(1024)S(1)}, s32[4096]{0:T(1024)}, u32[]{:S(2)}) copy-start(s32[4096]{0:T(1024)} %param.19) | copy-start | bytes 49156
Sparse Core Ops, SparseCore 0:
  69.0 23.5 all-reduce.6
  99.6 88.1 all-reduce.4
where the time goes:
time: 298 us; the launch traced here: 297 us
  blocking collectives  163 us (55%)
  waiting for transfers between devices  75.1 us (25%)
  matrix products  25.4 us (9%)
  between operations  14.8 us (5%)
  starting transfers between devices  9.85 us (3%)
  local copies, waits for them, and re-layouts  4.89 us (2%)
  other arithmetic  3.71 us (1%)
    psum x2, blocking collectives, on_device(): totals, chosen_logit = lax.psum((part_total, part_chosen), ('grp', 'exp'))  79.7 us
    psum x1, waiting for transfers between devices, on_device(): moe_slab = lax.psum(contrib, 'exp')  68.5 us
    all_gather x1, blocking collectives, on_device(): lax.all_gather(route_ids, 'exp', axis=0, tiled=True)  23.3 us
    all_gather x1, blocking collectives, on_device(): lax.all_gather(route_logits, 'exp', axis=0, tiled=True)  19.2 us
    all_gather x1, blocking collectives, on_device(): lax.all_gather(hidden, 'exp', axis=0, tiled=True)  18.4 us
    dot_general x1, matrix products, on_device(): jnp.dot(scaled, head_weight, preferred_element_type=jnp.float32)  13.7 us
    unnamed x1, blocking collectives  10.2 us
    all_gather x1, blocking collectives, on_device(): piece = lax.all_gather(residual, 'grp', axis=1, tiled=True)  6.51 us
  transfers between devices with their start and end apart: 5, of which 3 were waited for; matrix products, arithmetic and copies ran while one was open for 2% of the time, Pallas kernels for 0%

commit v1 on v0

--- a/solution.py
+++ b/solution.py
@@ -1,6 +1,10 @@
+import functools
+
 import jax
 import jax.numpy as jnp
 from jax import lax
+from jax.experimental import pallas as pl
+from jax.experimental.pallas import tpu as pltpu
 from jax.sharding import PartitionSpec as P
 
 TOPK = 8
@@ -12,7 +16,7 @@
 norm_eps = 1e-06
 
 
-def on_device(
+def on_device_general(
     hidden,
     route_ids,
     route_logits,
@@ -99,6 +103,528 @@
     return (vote_counts, own_ratio)
 
 
+MESH = pl.DeviceIdType.MESH
+LANES = 128
+FF_CHUNK = 512
+OUT_CHUNK = 512
+HEAD_ROWS = 512
+HEAD_CHUNK = 512
+VMEM_BYTES = 62 * 1024 * 1024
+
+
+def plane_order(plane, planes):
+    if planes != 4:
+        return [lax.rem(plane + t, planes) for t in range(planes)]
+    half = lax.div(plane, 2)
+    return [plane, plane + 1 - 2 * lax.rem(plane, 2), 2 - half, 3 - 3 * half]
+
+
+def fused_kernel(
+    groups,
+    experts,
+    hidden_ref,
+    ids_ref,
+    logits_ref,
+    sampled_ref,
+    gain_ref,
+    gate_hbm,
+    up_hbm,
+    down_hbm,
+    head_hbm,
+    votes_ref,
+    ratio_ref,
+    gate_w,
+    up_w,
+    down_w,
+    head_w,
+    row_f32,
+    row_stage,
+    rows_in,
+    rows_f32,
+    slab,
+    meta_out,
+    meta_in,
+    part_own,
+    part_out,
+    part_in,
+    active,
+    contrib,
+    contrib_in,
+    block_out,
+    residual,
+    scaled,
+    exps,
+    sums_out,
+    sums_in,
+    gu_sem,
+    down_sem,
+    head_sem,
+    rows_send,
+    rows_recv,
+    meta_send,
+    meta_recv,
+    part_send,
+    part_recv,
+    contrib_send,
+    contrib_recv,
+    block_send,
+    block_recv,
+    relay_send,
+    sums_send,
+    sums_recv,
+):
+    g = lax.axis_index("grp")
+    e = lax.axis_index("exp")
+    count = groups * experts
+    me = g * experts + e
+    width = slab.shape[1]
+    ff = part_own.shape[2]
+    model = residual.shape[1]
+    vocab_block = head_w.shape[1]
+    pieces = width // LANES
+
+    gu_copies = []
+    for c in range(ff // FF_CHUNK):
+        cols = pl.ds(c * FF_CHUNK, FF_CHUNK)
+        a = pltpu.make_async_copy(gate_hbm.at[0, :, cols], gate_w.at[:, cols], gu_sem.at[2 * c])
+        b = pltpu.make_async_copy(up_hbm.at[0, :, cols], up_w.at[:, cols], gu_sem.at[2 * c + 1])
+        a.start()
+        b.start()
+        gu_copies.append((a, b))
+    down_copy = pltpu.make_async_copy(down_hbm.at[0], down_w, down_sem.at[0])
+    down_copy.start()
+    head_copies = []
+    for c in range(model // HEAD_ROWS):
+        rows = pl.ds(c * HEAD_ROWS, HEAD_ROWS)
+        a = pltpu.make_async_copy(head_hbm.at[rows, :], head_w.at[rows, :], head_sem.at[c])
+        a.start()
+        head_copies.append(a)
+
+    def peer_of(k):
+        peer = lax.rem(me + k, count)
+        return peer, lax.div(peer, experts), lax.rem(peer, experts)
+
+    barrier = pltpu.get_barrier_semaphore()
+
+    def greet(k, carry):
+        peer, pg, pe = peer_of(k)
+        pl.semaphore_signal(barrier, inc=1, device_id=(pg, pe), device_id_type=MESH)
+        return carry
+
+    lax.fori_loop(1, count, greet, 0)
+
+    row = hidden_ref[...].astype(jnp.float32)
+    for c in range(model // LANES):
+        row_f32[c : c + 1, :] = row[:, c * LANES : (c + 1) * LANES]
+    for h in range(groups):
+        row_stage[h] = row_f32[h * pieces : (h + 1) * pieces, :].astype(jnp.bfloat16)
+    lane = lax.broadcasted_iota(jnp.int32, (1, LANES), 1)
+    scores = logits_ref[...].astype(jnp.float32)
+    shifted = jnp.exp(scores - jnp.max(scores, axis=1, keepdims=True))
+    mixing = shifted / jnp.sum(shifted, axis=1, keepdims=True)
+    ids = ids_ref[...]
+    meta = jnp.where(lane == experts, sampled_ref[...].astype(jnp.float32), 0.0)
+    for k in range(ids.shape[1]):
+        meta = meta + jnp.where(lane == ids[:, k : k + 1], mixing[:, k : k + 1], 0.0)
+    meta_out[...] = meta
+    meta_in[me] = meta
+    rows_in[me] = row_stage[g]
+
+    pl.semaphore_wait(barrier, count - 1)
+
+    def rows_copy(k, sender):
+        peer, pg, pe = peer_of(k)
+        slot = me if sender else peer
+        return pltpu.make_async_remote_copy(
+            src_ref=row_stage.at[pg],
+            dst_ref=rows_in.at[slot],
+            send_sem=rows_send.at[k],
+            recv_sem=rows_recv.at[slot],
+            device_id=(pg, pe),
+            device_id_type=MESH,
+        )
+
+    def meta_copy(k, sender):
+        peer, pg, pe = peer_of(k)
+        slot = me if sender else peer
+        return pltpu.make_async_remote_copy(
+            src_ref=meta_out,
+            dst_ref=meta_in.at[slot],
+            send_sem=meta_send.at[k],
+            recv_sem=meta_recv.at[slot],
+            device_id=(pg, pe),
+            device_id_type=MESH,
+        )
+
+    def each(low, high, action):
+        def step(k, carry):
+            action(k)
+            return carry
+
+        lax.fori_loop(low, high, step, 0)
+
+    each(1, count, lambda k: rows_copy(k, True).start())
+    each(1, count, lambda k: meta_copy(k, True).start())
+    each(1, count, lambda k: rows_copy(k, False).wait_recv())
+
+    for m in range(count):
+        rows_f32[m * pieces : (m + 1) * pieces, :] = rows_in[m].astype(jnp.float32)
+    for c in range(pieces):
+        slab[:, c * LANES : (c + 1) * LANES] = rows_f32[
+            pl.ds(c, count, stride=pieces), :
+        ].astype(jnp.bfloat16)
+
+    def part_copy(c, k, sender):
+        og = lax.rem(g + k, groups)
+        slot = g if sender else og
+        return pltpu.make_async_remote_copy(
+            src_ref=part_out.at[c],
+            dst_ref=part_in.at[slot, c],
+            send_sem=part_send.at[k, c],
+            recv_sem=part_recv.at[slot, c],
+            device_id=(og, e),
+            device_id_type=MESH,
+        )
+
+    for c in range(ff // FF_CHUNK):
+        cols = slice(c * FF_CHUNK, (c + 1) * FF_CHUNK)
+        for i, (copy, weight) in enumerate(zip(gu_copies[c], (gate_w, up_w))):
+            copy.wait()
+            value = jnp.dot(slab[...], weight[:, cols], preferred_element_type=jnp.float32)
+            part_own[i, :, cols] = value
+            part_out[c, i] = value.astype(jnp.bfloat16)
+        for k in range(1, groups):
+            part_copy(c, k, True).start()
+
+    each(1, count, lambda k: meta_copy(k, False).wait_recv())
+    metas = jnp.concatenate([meta_in[m] for m in range(count)], axis=0)
+    wide_lane = lax.broadcasted_iota(jnp.int32, (count, LANES), 1)
+    share = jnp.sum(jnp.where(wide_lane == e, metas, 0.0), axis=1, keepdims=True)
+    wanted = jnp.sum(jnp.where(wide_lane == experts, metas, 0.0), axis=1, keepdims=True)
+
+    for c in range(ff // FF_CHUNK):
+        cols = slice(c * FF_CHUNK, (c + 1) * FF_CHUNK)
+        gate, upward = part_own[0, :, cols], part_own[1, :, cols]
+        for k in range(1, groups):
+            part_copy(c, k, False).wait_recv()
+            og = lax.rem(g + k, groups)
+            gate = gate + part_in[og, c, 0].astype(jnp.float32)
+            upward = upward + part_in[og, c, 1].astype(jnp.float32)
+        active[:, cols] = (gate / (1.0 + jnp.exp(-gate)) * upward).astype(jnp.bfloat16)
+
+    quad = OUT_CHUNK // LANES
+    plane, corner = lax.div(e, quad), lax.rem(e, quad)
+    parity = lax.rem(corner, 2)
+    row_in_plane = lax.div(corner, 2)
+    order = plane_order(plane, experts // quad)
+
+    def contrib_copy(t, p, sender):
+        there = lax.rem(corner + p, quad)
+        oe = order[t] * quad + there
+        slot = e if sender else oe
+        return pltpu.make_async_remote_copy(
+            src_ref=contrib.at[t * quad + there],
+            dst_ref=contrib_in.at[slot],
+            send_sem=contrib_send.at[t * quad + p],
+            recv_sem=contrib_recv.at[slot],
+            device_id=(g, oe),
+            device_id_type=MESH,
+        )
+
+    steps = len(order)
+    down_copy.wait()
+    for t in reversed(range(steps)):
+        cols = pl.ds(pl.multiple_of(order[t] * OUT_CHUNK, OUT_CHUNK), OUT_CHUNK)
+        value = jnp.dot(active[...], down_w[:, cols], preferred_element_type=jnp.float32)
+        value = value.astype(jnp.bfloat16).astype(jnp.float32) * share
+        value = value.astype(jnp.bfloat16)
+        for p in range(quad):
+            contrib[t * quad + p] = value[:, p * LANES : (p + 1) * LANES]
+        for p in range(0 if t else 1, quad):
+            contrib_copy(t, p, True).start()
+    mine = pl.ds(pl.multiple_of(e * LANES, LANES), LANES)
+    total = slab[:, mine].astype(jnp.float32)
+    moe = contrib[corner].astype(jnp.float32)
+    for t in range(steps):
+        for p in range(0 if t else 1, quad):
+            contrib_copy(t, p, False).wait_recv()
+            there = order[t] * quad + lax.rem(corner + p, quad)
+            moe = moe + contrib_in[there].astype(jnp.float32)
+    block = (total + moe).astype(jnp.bfloat16)
+    block_out[...] = block
+
+    def columns_of(slot):
+        return pl.ds(pl.multiple_of(slot * LANES, LANES), LANES)
+
+    def block_copy(t, a, b, sender):
+        og = lax.rem(g + a, groups)
+        oe = order[t] * quad + 2 * lax.rem(row_in_plane + b, quad // 2) + parity
+        slot = me if sender else og * experts + oe
+        n = (t * groups + a) * (quad // 2) + b
+        return pltpu.make_async_remote_copy(
+            src_ref=block_out,
+            dst_ref=residual.at[:, columns_of(slot)],
+            send_sem=block_send.at[n],
+            recv_sem=block_recv.at[slot],
+            device_id=(og, oe),
+            device_id_type=MESH,
+        )
+
+    def relay_copy(t, a, b, sender):
+        og = lax.rem(g + a, groups)
+        pair = order[t] * quad + 2 * lax.rem(row_in_plane + b, quad // 2)
+        slot = og * experts + pair + (parity if sender else 1 - parity)
+        n = (t * groups + a) * (quad // 2) + b
+        own = sender and (t, a, b) == (0, 0, 0)
+        return pltpu.make_async_remote_copy(
+            src_ref=block_out if own else residual.at[:, columns_of(slot)],
+            dst_ref=residual.at[:, columns_of(slot)],
+            send_sem=relay_send.at[n],
+            recv_sem=block_recv.at[slot],
+            device_id=(g, e + 1 - 2 * parity),
+            device_id_type=MESH,
+        )
+
+    spots = [(a, b) for a in range(groups) for b in range(quad // 2)]
+    for t in reversed(range(steps)):
+        for a, b in spots:
+            if (t, a, b) != (0, 0, 0):
+                block_copy(t, a, b, True).start()
+    relay_copy(0, 0, 0, True).start()
+    residual[:, columns_of(me)] = block
+
+    def relay(t):
+        for a, b in spots:
+            if (t, a, b) != (0, 0, 0):
+                block_copy(t, a, b, False).wait_recv()
+                relay_copy(t, a, b, True).start()
+
+    first = wanted - (me * vocab_block).astype(jnp.float32)
+    depth = groups * OUT_CHUNK
+    squares = jnp.zeros((count, LANES), jnp.float32)
+    zero = jnp.zeros((count, LANES), jnp.float32)
+    for copy in head_copies:
+        copy.wait()
+    relay(0)
+    for t in range(steps):
+        if t + 1 < steps:
+            relay(t + 1)
+        for a, b in spots:
+            relay_copy(t, a, b, False).wait_recv()
+        starts = [pl.multiple_of(h * width + order[t] * OUT_CHUNK, OUT_CHUNK) for h in range(groups)]
+        for h in range(groups):
+            for p in range(quad):
+                cols = pl.ds(pl.multiple_of(starts[h] + p * LANES, LANES), LANES)
+                value = residual[:, cols].astype(jnp.float32)
+                squares = squares + value * value
+                at = t * depth + h * OUT_CHUNK + p * LANES
+                scaled[:, at : at + LANES] = (value * gain_ref[:, cols]).astype(jnp.bfloat16)
+
+        def product(cols, t=t, starts=starts):
+            value = None
+            for h in range(groups):
+                at = t * depth + h * OUT_CHUNK
+                part = jnp.dot(
+                    scaled[:, at : at + OUT_CHUNK],
+                    head_w[pl.ds(starts[h], OUT_CHUNK), cols],
+                    preferred_element_type=jnp.float32,
+                )
+                value = part if value is None else value + part
+            return value if t == 0 else value + exps[:, cols]
+
+        if t + 1 < steps:
+
+            def gather_step(c, carry, product=product):
+                cols = pl.ds(pl.multiple_of(c * HEAD_CHUNK, HEAD_CHUNK), HEAD_CHUNK)
+                exps[:, cols] = product(cols)
+                return carry
+
+            lax.fori_loop(0, vocab_block // HEAD_CHUNK, gather_step, 0)
+            continue
+
+        mean = jnp.sum(squares, axis=1, keepdims=True) / model
+        inverse = 1.0 / jnp.sqrt(mean + norm_eps)
+
+        def head_step(c, carry, product=product, inverse=inverse):
+            sums, picked = carry
+            cols = pl.ds(pl.multiple_of(c * HEAD_CHUNK, HEAD_CHUNK), HEAD_CHUNK)
+            value = jnp.clip(product(cols) * inverse, -clip_bound, clip_bound)
+            grown = jnp.exp(value)
+            exps[:, cols] = grown
+            column = lax.broadcasted_iota(jnp.int32, (count, HEAD_CHUNK), 1) + c * HEAD_CHUNK
+            owned = jnp.where(column.astype(jnp.float32) == first, value, 0.0)
+            for p in range(HEAD_CHUNK // LANES):
+                part = slice(p * LANES, (p + 1) * LANES)
+                sums = sums + grown[:, part]
+                picked = picked + owned[:, part]
+            return sums, picked
+
+        sums, picked = lax.fori_loop(0, vocab_block // HEAD_CHUNK, head_step, (zero, zero))
+    diagonal = lax.broadcasted_iota(jnp.int32, (count, LANES), 0) == wide_lane
+    for i, value in enumerate((sums, picked)):
+        column = jnp.sum(value, axis=1, keepdims=True)
+        sums_out[i : i + 1, :] = jnp.sum(jnp.where(diagonal, column, 0.0), axis=0, keepdims=True)
+
+    def sums_copy(k, sender):
+        peer, pg, pe = peer_of(k)
+        slot = me if sender else peer
+        return pltpu.make_async_remote_copy(
+            src_ref=sums_out,
+            dst_ref=sums_in.at[slot],
+            send_sem=sums_send.at[k],
+            recv_sem=sums_recv.at[slot],
+            device_id=(pg, pe),
+            device_id_type=MESH,
+        )
+
+    each(1, count, lambda k: sums_copy(k, True).start())
+    sums_in[me] = sums_out[...]
+    each(1, count, lambda k: rows_copy(k, True).wait_send())
+    each(1, count, lambda k: meta_copy(k, True).wait_send())
+    for c in range(ff // FF_CHUNK):
+        for k in range(1, groups):
+            part_copy(c, k, True).wait_send()
+    for t in range(steps):
+        for p in range(0 if t else 1, quad):
+            contrib_copy(t, p, True).wait_send()
+        for a, b in spots:
+            if (t, a, b) != (0, 0, 0):
+                block_copy(t, a, b, True).wait_send()
+            relay_copy(t, a, b, True).wait_send()
+    each(1, count, lambda k: sums_copy(k, False).wait_recv())
+    both = sums_in[0]
+    for k in range(1, count):
+        both = both + sums_in[k]
+    totals, chosen = both[0:1], both[1:2]
+    ratio = chosen - jnp.log(jnp.where(lane < count, totals, 1.0) / (vocab_block * count))
+    ratio = jnp.sum(jnp.where(lane == me, ratio, 0.0), axis=1, keepdims=True)
+    ratio_ref[...] = jnp.broadcast_to(ratio, ratio_ref.shape)
+    weight = jnp.sum(jnp.where(diagonal, totals, 0.0), axis=1, keepdims=True)
+    weight = vocab_block / weight
+    for c in range(vocab_block // HEAD_CHUNK):
+        cols = slice(c * HEAD_CHUNK, (c + 1) * HEAD_CHUNK)
+        votes_ref[:, cols] = jnp.sum(exps[:, cols] * weight, axis=0, keepdims=True)
+    each(1, count, lambda k: sums_copy(k, True).wait_send())
+
+
+def fused(
+    groups,
+    experts,
+    hidden,
+    route_ids,
+    route_logits,
+    sampled,
+    norm_gain,
+    gate_weight,
+    up_weight,
+    down_weight,
+    head_weight,
+    noise_steps,
+):
+    count = groups * experts
+    width, ff = gate_weight.shape[1:]
+    model, vocab_block = head_weight.shape
+    pieces = width // LANES
+    chunks = ff // FF_CHUNK
+    bf16, f32 = jnp.bfloat16, jnp.float32
+    vmem = pl.BlockSpec(memory_space=pltpu.VMEM)
+    hbm = pl.BlockSpec(memory_space=pl.ANY)
+    dma = pltpu.SemaphoreType.DMA
+    votes, ratio = pl.pallas_call(
+        functools.partial(fused_kernel, groups, experts),
+        out_shape=(
+            jax.ShapeDtypeStruct((1, vocab_block), f32),
+            jax.ShapeDtypeStruct((1, LANES), f32),
+        ),
+        in_specs=[vmem] * 5 + [hbm] * 4,
+        out_specs=(vmem, vmem),
+        scratch_shapes=[
+            pltpu.VMEM((width, ff), bf16),
+            pltpu.VMEM((width, ff), bf16),
+            pltpu.VMEM((ff, width), bf16),
+            pltpu.VMEM((model, vocab_block), bf16),
+            pltpu.VMEM((model // LANES, LANES), f32),
+            pltpu.VMEM((groups, pieces, LANES), bf16),
+            pltpu.VMEM((count, pieces, LANES), bf16),
+            pltpu.VMEM((count * pieces, LANES), f32),
+            pltpu.VMEM((count, width), bf16),
+            pltpu.VMEM((1, LANES), f32),
+            pltpu.VMEM((count, 1, LANES), f32),
+            pltpu.VMEM((2, count, ff), f32),
+            pltpu.VMEM((chunks, 2, count, FF_CHUNK), bf16),
+            pltpu.VMEM((groups, chunks, 2, count, FF_CHUNK), bf16),
+            pltpu.VMEM((count, ff), bf16),
+            pltpu.VMEM((experts, count, LANES), bf16),
+            pltpu.VMEM((experts, count, LANES), bf16),
+            pltpu.VMEM((count, LANES), bf16),
+            pltpu.VMEM((count, model), bf16),
+            pltpu.VMEM((count, model), bf16),
+            pltpu.VMEM((count, vocab_block), f32),
+            pltpu.VMEM((2, LANES), f32),
+            pltpu.VMEM((count, 2, LANES), f32),
+            dma((2 * chunks,)),
+            dma((1,)),
+            dma((model // HEAD_ROWS,)),
+            dma((count,)),
+            dma((count,)),
+            dma((count,)),
+            dma((count,)),
+            dma((groups, chunks)),
+            dma((groups, chunks)),
+            dma((experts,)),
+            dma((experts,)),
+            dma((count,)),
+            dma((count,)),
+            dma((count,)),
+            dma((count,)),
+            dma((count,)),
+        ],
+        compiler_params=pltpu.CompilerParams(
+            collective_id=0, has_side_effects=True, vmem_limit_bytes=VMEM_BYTES
+        ),
+    )(
+        hidden,
+        route_ids,
+        route_logits,
+        sampled.reshape(1, 1),
+        norm_gain.reshape(1, model),
+        gate_weight,
+        up_weight,
+        down_weight,
+        head_weight,
+    )
+    vote_counts = votes.reshape(vocab_block) + noise_steps.astype(f32) * noise_step
+    return (vote_counts, ratio[0, :1])
+
+
+def on_device(hidden, route_ids, route_logits, sampled, norm_gain, *weights):
+    groups, experts = lax.axis_size("grp"), lax.axis_size("exp")
+    count = groups * experts
+    width, ff = weights[0].shape[1:]
+    model, vocab_block = weights[3].shape
+    held = 2 * (3 * width * ff + model * vocab_block)
+    fits = (
+        hidden.shape[0] == 1
+        and weights[0].shape[0] == 1
+        and width == experts * LANES
+        and model == groups * width
+        and width % (16 * LANES) == 0
+        and ff % FF_CHUNK == 0
+        and width % OUT_CHUNK == 0
+        and model % HEAD_ROWS == 0
+        and vocab_block % HEAD_CHUNK == 0
+        and count % 16 == 0
+        and experts % (OUT_CHUNK // LANES) == 0
+        and OUT_CHUNK // LANES % 2 == 0
+        and count <= LANES
+        and held <= 54 * 1024 * 1024
+    )
+    whole = (hidden, route_ids, route_logits, sampled, norm_gain, *weights)
+    if fits:
+        return fused(groups, experts, *whole)
+    return on_device_general(*whole)
+
+
 def solution(mesh):
     placed = (
         P(("grp", "exp"), None),

time: 298 us -> 53.9 us (0.18)
  blocking collectives: 163 us -> 0 us
  waiting for transfers between devices: 75.1 us -> 0 us
  Pallas kernels: 0 us -> 49.1 us
  matrix products: 25.4 us -> 0 us
  between operations: 14.8 us -> 3.06 us
  starting transfers between devices: 9.85 us -> 0 us
  local copies, waits for them, and re-layouts: 4.89 us -> 0.01 us
    psum x2 -> x0, blocking collectives: 79.7 us -> none  [on_device(): totals, chosen_logit = lax.psum((part_total, part_chosen), ('grp', 'exp'))]
    psum x2 -> x0, waiting for transfers between devices: 68.6 us -> none  [the longest x1 68.5 us: on_device(): moe_slab = lax.psum(contrib, 'exp')]
    all_gather x4 -> x0, blocking collectives: 67.4 us -> none  [the longest x1 23.3 us: on_device(): lax.all_gather(route_ids, 'exp', axis=0, tiled=True)]
    pallas_call x0 -> x1, Pallas kernels: none -> 49.1 us  [fused(): pl.pallas_call(functools.partial(fused_kernel, groups, experts), out_shap...]
    dot_general x5 -> x0, matrix products: 25.4 us -> none  [the longest x1 13.7 us: on_device(): jnp.dot(scaled, head_weight, preferred_element_type=jnp.float32)]
    unnamed x1 -> x0, blocking collectives: 10.2 us -> none
    all_to_all x3 -> x0, starting transfers between devices: 9.77 us -> none  [the longest x1 3.38 us: on_device(): lax.all_to_all(pieces, 'grp', split_axis=1, concat_axis=0, tiled=True)]
    all_to_all x3 -> x0, waiting for transfers between devices: 6.52 us -> none  [the longest x1 3.67 us: on_device(): lax.all_to_all(sampled_spread, 'grp', split_axis=1, concat_axis=0, tiled=...]
  transfers between devices with their start and end apart: 5 -> 0, of which waited for: 3 -> 0; matrix products, arithmetic and copies ran while one was open for 2% -> 0% of each run, Pallas kernels for 0% -> 0%
where the time goes in v1:
time: 53.9 us; the launch traced here: 53.5 us
  Pallas kernels  49.1 us (91%)
  between operations  3.06 us (6%)
  other arithmetic  1.33 us (2%)
    pallas_call x1, Pallas kernels, fused(): pl.pallas_call(functools.partial(fused_kernel, groups, experts), out_shap...  49.1 us
    add x1, other arithmetic, fused(): votes.reshape(vocab_block) + noise_steps.astype(f32) * noise_step  1.33 us

profile of v1, /device:TPU:0, one launch (start us, length us, event | category | flops | bytes accessed | tf_op | source)
XLA Modules:
  0.0 53.5 jit_solution(7016069098268882602)
XLA Ops:
  1.3 0.0 copy-start
  1.3 49.1 %shard_map.113 = (f32[1,4096]{1,0:T(1,128)}, f32[1,128]{1,0:T(1,128)}) custom-call(bf16[1,4096]{1,0:T(2,128)(2,1)} %hidden_ref.1, s32[1,8]{1,0:T(1,128)} %ids_ref.1, bf16[1,8]{1,0:T(2,128)(2,1)} %logits_ref.1, s32[1,1]{1,0:T(1,128)} %bitcast.5.sampled_ref, f32[1,4096]{1,0:T(1,128)} %bitcast.6, bf16[1,2048,1536]{2,1,0:T(8,128)(2,1)} %gate_hbm.1, ...), custom_call_target="tpu_custom_call" | custom-call | tf_op jit(solution)/shard_map/pallas_call | solution.py:533
  50.4 0.0 copy-done
  50.4 1.3 %multiply_add_fusion = f32[4096]{0:T(1024)} fusion(f32[4096]{0:T(1024)} %bitcast.7, s32[4096]{0:T(1024)S(1)} %copy-done), kind=kLoop, calls=%fused_computation | loop fusion | flops 12288 | bytes 49152 | tf_op jit(solution)/shard_map/add | solution.py:596
Async XLA Ops:
  1.3 49.2 %copy-start = (s32[4096]{0:T(1024)S(1)}, s32[4096]{0:T(1024)}, u32[]{:S(2)}) copy-start(s32[4096]{0:T(1024)} %param.19) | copy-start | bytes 49156
